TPU v7x, 512 devices: a whole 4x8x8 slice. The times are simulated.
512 devices in a mesh: src: 16 (over z_hi, x, core), rows: 32 (over z_lo, y).
Axes of the slice: x: 4, y: 8, z: 8 (z_hi: 2, z_lo: 4; z = z_hi * 4 + z_lo), core: 2. Of those that a mesh axis runs over, the one named last changes fastest.
Arguments:
- mask_param: float32 [512, 8192], P('rows'), may hold values from -6 to 6
- target: int32 [512, 8192], P('rows', 'src'), may hold values 0 or 1
- source_weight: float32 [16], replicated, may hold values from 0.25 to 4
- row_shift: int32 [16], replicated, may hold values from -8 to 8
- col_shift: int32 [16], replicated, may hold values from -32 to 32
Outputs:
- mask_grad: float32 [512, 8192], P('rows', 'src')
All inputs are finite; a program needn't handle non-finite values. No bound on the sum of `target` on one device may be relied on, other than what follows from the above.
Results may differ from a plain program's by a relative error of at most 0.0003.
Values sent between devices are 32-bit elements; how exact they have to be, the bound alone decides.
No kernel may reach another device: no remote copies, remote signals or barrier semaphores. Data moves between devices by JAX's collectives and lax.ppermute only.
A program may use at most 64 MiB of HBM per device.

v0:
```python
import math
import jax
import jax.numpy as jnp
from jax import lax
from jax.sharding import PartitionSpec as P

steepness = 250.0
threshold_level = 0.25
loss_weight = 8.0
highest = lax.Precision.HIGHEST


def product(matrix_left, matrix_right):
    return jnp.dot(matrix_left, matrix_right, precision=highest, preferred_element_type=jnp.float32)


def product_nt(matrix_left, matrix_right):
    return lax.dot_general(
        matrix_left,
        matrix_right,
        (((1,), (1,)), ((), ())),
        precision=highest,
        preferred_element_type=jnp.float32,
    )


def product_tn(matrix_left, matrix_right):
    return lax.dot_general(
        matrix_left,
        matrix_right,
        (((0,), (0,)), ((), ())),
        precision=highest,
        preferred_element_type=jnp.float32,
    )


def centered(number):
    return jnp.arange(number, dtype=jnp.int32) - number // 2


def phases(frequency, position, period):
    angles = jnp.mod(position[:, None] * frequency[None, :], period).astype(jnp.float32) * (
        2.0 * math.pi / period
    )
    return (jnp.cos(angles), jnp.sin(angles))


def pupil_mask(row_offset, col_offset, band_rows, band_cols):
    radius_rows = band_rows // 4
    radius_cols = band_cols // 4
    row_term = (centered(band_rows) + row_offset) ** 2 * (radius_cols * radius_cols)
    col_term = (centered(band_cols) + col_offset) ** 2 * (radius_rows * radius_rows)
    limit_value = (radius_rows * radius_cols) ** 2
    return (row_term[:, None] + col_term[None, :] <= limit_value).astype(jnp.float32)


def columns_forward(real_part, imag_part, column_start, band_cols, total_columns):
    row_count, col_width = real_part.shape
    block_width = min(512, col_width)
    block_count = col_width // block_width
    frequency = centered(band_cols)
    base_cos, base_sin = phases(frequency, jnp.arange(block_width, dtype=jnp.int32), total_columns)
    starts = column_start + block_width * jnp.arange(block_count, dtype=jnp.int32)
    twist_cos, twist_sin = phases(frequency, starts, total_columns)
    stack_rows = row_count * block_count
    if imag_part is None:
        flat_real = real_part.reshape(stack_rows, block_width)
        part_real = product(flat_real, base_cos)
        part_imag = -product(flat_real, base_sin)
    else:
        stacked = jnp.concatenate(
            [
                real_part.reshape(stack_rows, block_width),
                imag_part.reshape(stack_rows, block_width),
            ],
            axis=0,
        )
        with_cos = product(stacked, base_cos)
        with_sin = product(stacked, base_sin)
        part_real = with_cos[:stack_rows] + with_sin[stack_rows:]
        part_imag = with_cos[stack_rows:] - with_sin[:stack_rows]
    part_real = part_real.reshape(row_count, block_count, band_cols)
    part_imag = part_imag.reshape(row_count, block_count, band_cols)
    out_real = jnp.sum(part_real * twist_cos + part_imag * twist_sin, axis=1)
    out_imag = jnp.sum(part_imag * twist_cos - part_real * twist_sin, axis=1)
    return (out_real, out_imag)


def rows_forward(real_part, imag_part, row_start, band_rows, total_rows):
    position = row_start + jnp.arange(real_part.shape[0], dtype=jnp.int32)
    row_cos, row_sin = phases(centered(band_rows), position, total_rows)
    out_real = product_tn(row_cos, real_part) + product_tn(row_sin, imag_part)
    out_imag = product_tn(row_cos, imag_part) - product_tn(row_sin, real_part)
    return (out_real, out_imag)


def rows_inverse(real_part, imag_part, row_start, row_count, total_rows):
    position = row_start + jnp.arange(row_count, dtype=jnp.int32)
    row_cos, row_sin = phases(centered(real_part.shape[0]), position, total_rows)
    out_real = product(row_cos, real_part) - product(row_sin, imag_part)
    out_imag = product(row_cos, imag_part) + product(row_sin, real_part)
    return (out_real, out_imag)


def columns_inverse(real_part, imag_part, column_start, width_out, total_columns):
    row_count, band_cols = real_part.shape
    block_width = min(512, width_out)
    block_count = width_out // block_width
    frequency = centered(band_cols)
    base_cos, base_sin = phases(frequency, jnp.arange(block_width, dtype=jnp.int32), total_columns)
    starts = column_start + block_width * jnp.arange(block_count, dtype=jnp.int32)
    twist_cos, twist_sin = phases(frequency, starts, total_columns)
    turned_real = real_part[:, None, :] * twist_cos - imag_part[:, None, :] * twist_sin
    turned_imag = real_part[:, None, :] * twist_sin + imag_part[:, None, :] * twist_cos
    stack_rows = row_count * block_count
    stacked = jnp.concatenate(
        [turned_real.reshape(stack_rows, band_cols), turned_imag.reshape(stack_rows, band_cols)],
        axis=0,
    )
    with_cos = product_nt(stacked, base_cos)
    with_sin = product_nt(stacked, base_sin)
    field_real = (with_cos[:stack_rows] - with_sin[stack_rows:]).reshape(row_count, width_out)
    field_imag = (with_sin[:stack_rows] + with_cos[stack_rows:]).reshape(row_count, width_out)
    return (field_real, field_imag)


def resist_slope(intensity, target):
    resist = jax.nn.sigmoid(steepness * (intensity - threshold_level))
    return (
        2.0
        * loss_weight
        * (resist - target.astype(jnp.float32))
        * steepness
        * resist
        * (1.0 - resist)
    )


def local(mask_param, target, source_weight, row_shift, col_shift):
    row_block, total_columns = mask_param.shape
    src_count = lax.axis_size("src")
    src_index = lax.axis_index("src")
    row_index = lax.axis_index("rows")
    total_rows = row_block * lax.axis_size("rows")
    band_rows = total_rows // 16
    band_cols = total_columns // 64
    col_share = total_columns // src_count
    local_points = source_weight.shape[0] // src_count
    row_start = row_index * row_block
    share_start = src_index * col_share
    unit_scale = 1.0 / math.sqrt(total_rows * total_columns)
    opening = jax.nn.sigmoid(mask_param)
    all_weights = source_weight / jnp.sum(source_weight)
    col_real, col_imag = columns_forward(opening, None, 0, band_cols, total_columns)
    part_real, part_imag = rows_forward(col_real, col_imag, row_start, band_rows, total_rows)
    band_real, band_imag = lax.psum((part_real * unit_scale, part_imag * unit_scale), "rows")
    my_weights = lax.dynamic_slice_in_dim(all_weights, src_index * local_points, local_points)
    my_rows = lax.dynamic_slice_in_dim(row_shift, src_index * local_points, local_points)
    my_cols = lax.dynamic_slice_in_dim(col_shift, src_index * local_points, local_points)
    source_point = 0
    opened = pupil_mask(my_rows[source_point], my_cols[source_point], band_rows, band_cols)
    head_real, head_imag = rows_inverse(
        band_real * opened * unit_scale,
        band_imag * opened * unit_scale,
        row_start,
        row_block,
        total_rows,
    )
    field_real, field_imag = columns_inverse(head_real, head_imag, 0, total_columns, total_columns)
    intensity_part = my_weights[source_point] * (field_real * field_real + field_imag * field_imag)
    field_list = [(field_real, field_imag)]
    pupil_list = [opened]
    intensity = lax.psum_scatter(intensity_part, "src", scatter_dimension=1, tiled=True)
    slope_share = resist_slope(intensity, target)
    slope = lax.all_gather(slope_share, "src", axis=1, tiled=True)
    source_point = 0
    field_real, field_imag = field_list[source_point]
    factor = 2.0 * my_weights[source_point] * slope
    cot_real, cot_imag = columns_forward(
        factor * field_real, factor * field_imag, 0, band_cols, total_columns
    )
    back_real, back_imag = rows_forward(cot_real, cot_imag, row_start, band_rows, total_rows)
    adjoint_real = pupil_list[source_point] * back_real
    adjoint_imag = pupil_list[source_point] * back_imag
    adjoint_real, adjoint_imag = lax.psum(
        (adjoint_real * unit_scale, adjoint_imag * unit_scale), ("src", "rows")
    )
    head_real, head_imag = rows_inverse(
        adjoint_real * unit_scale, adjoint_imag * unit_scale, row_start, row_block, total_rows
    )
    grad_real, grad_imag = columns_inverse(
        head_real, head_imag, share_start, col_share, total_columns
    )
    own_open = lax.dynamic_slice_in_dim(opening, share_start, col_share, 1)
    return grad_real * own_open * (1.0 - own_open)


def solution(mesh):
    placed = (P("rows", None), P("rows", "src"), P(), P(), P())
    return jax.shard_map(
        local, mesh=mesh, in_specs=placed, out_specs=P("rows", "src"), check_vma=False
    )
```

profile of v0, /device:TPU:1, one launch (start us, length us, event | category | flops | bytes accessed | tf_op | source)
XLA Modules:
  0.0 408.0 jit_solution(5263452524671067689)
XLA Ops:
  6.5 0.0 reduce-scatter.2.cloned.1.call-start
  6.5 1.2 add_divide_fusion
  7.7 0.1 reshape.193
  7.8 0.1 fusion.73
  8.0 1.5 convolution_negate_fusion
  9.5 0.3 copy.6
  9.9 1.6 add_reduce_fusion.1
  11.4 0.3 fusion.86
  11.8 0.3 fusion.83
  12.1 0.3 fusion.7
  12.4 0.3 fusion.6
  12.8 0.0 copy-start.1
  12.8 0.6 copy-done.1
  13.5 0.6 dynamic_slice.13
  14.0 0.0 copy-start.2
  14.0 0.7 multiply_multiply_fusion.2
  14.7 0.0 copy-done.2
  14.7 0.6 dynamic_slice.12
  15.3 0.7 multiply_multiply_fusion.3
  16.0 128.9 %all-reduce.1 = (f32[32,128]{1,0:T(8,128)S(1)}, f32[32,128]{1,0:T(8,128)S(1)}) all-reduce(f32[32,128]{1,0:T(8,128)S(1)} %fusion.6, f32[32,128]{1,0:T(8,128)S(1)} %fusion.7), channel_id=1, replica_groups=mesh['src'=16,'rows'=32] {'rows'}, use_global_device_ids=true, to_apply=%region_4.5 | all-reduce | flops 8192 | bytes 65536 | tf_op jit(solution)/shard_map/psum | solution.py:156
  144.9 0.2 fusion.37
  145.1 0.3 fusion.38
  145.4 0.3 convolution_subtract_fusion.4
  145.6 0.3 convolution_add_fusion.3
  145.9 1.9 fusion.16
  147.9 1.9 fusion.17
  149.8 0.2 slice_add_fusion
  150.0 0.1 reshape.195
  150.2 0.0 copy-start.3
  150.2 0.1 reshape.196
  150.3 0.5 copy-done.3
  150.8 0.6 reduce_sum.45
  151.4 0.6 broadcast_divide_fusion
  152.1 0.6 dynamic_slice.14
  152.7 1.5 add_multiply_fusion
  154.2 0.0 copy-start
  154.2 0.0 reduce-scatter.2.cloned.1.call-update
  154.8 0.1 fusion.123
  154.9 107.6 %reduce-scatter.2.cloned.1.call-done = f32[16,512]{1,0:T(8,128)} async-done(((f32[16,8192]{1,0:T(8,128)}), f32[16,512]{1,0:T(8,128)}) %reduce-scatter.2.cloned.1.call-update) | async-done | bytes 32784 | tf_op jit(solution)/shard_map/reduce_scatter | solution.py:173
  262.5 0.0 copy-done
  262.5 0.8 subtract_multiply_fusion
  263.3 30.5 %all_gather.3 = f32[16,8192]{1,0:T(8,128)S(1)} all-gather(f32[16,512]{1,0:T(8,128)S(1)} %subtract_multiply_fusion), channel_id=1, replica_groups=mesh['src'=16,'rows'=32] {'src'}, dimensions={1}, use_global_device_ids=true | all-gather | bytes 557056 | tf_op jit(solution)/shard_map/all_gather | solution.py:175
  293.8 0.1 multiply_multiply_fusion
  293.9 0.1 reshape.197
  294.1 0.1 reshape.198
  294.2 1.9 fusion.22
  296.1 1.9 fusion.27
  298.1 0.1 add_reduce_fusion
  298.2 0.3 fusion.80
  298.5 0.3 fusion.77
  298.8 0.3 fusion.5
  299.2 0.3 fusion.3
  299.5 97.3 %all-reduce = (f32[32,128]{1,0:T(8,128)S(1)}, f32[32,128]{1,0:T(8,128)S(1)}) all-reduce(f32[32,128]{1,0:T(8,128)S(1)} %fusion.3, f32[32,128]{1,0:T(8,128)S(1)} %fusion.5), channel_id=1, replica_groups=mesh['src'=16,'rows'=32] {'src','rows'}, use_global_device_ids=true, to_apply=%region_9.10 | all-reduce | flops 8192 | bytes 65536 | tf_op jit(solution)/shard_map/psum | solution.py:185
  396.9 0.3 fusion.35
  397.1 0.3 fusion.31
  397.4 0.3 convolution_subtract_fusion.3
  397.6 0.3 multiply_add_fusion.1
  397.9 1.3 fusion.20
  399.2 1.9 fusion.1
  (7 shorter events, 0.1 us)
Async XLA Ops:
  6.5 256.0 %reduce-scatter.2.cloned.1.call-start = ((), (), s32[]{:S(2)}) async-start(), calls=%async_computation.1 | async-start | bytes 557056 | tf_op jit(solution)/shard_map/reduce_scatter | solution.py:173
  12.8 0.7 copy-start.1
  14.0 0.7 copy-start.2
  150.2 0.7 copy-start.3
  154.2 108.4 %copy-start = (s32[16,512]{1,0:T(8,128)S(1)}, s32[16,512]{1,0:T(8,128)}, u32[]{:S(2)}) copy-start(s32[16,512]{1,0:T(8,128)} %param.6) | copy-start | bytes 98308
Sparse Core Ops, SparseCore 0:
  154.3 108.1 reduce-scatter.1
where the time goes:
time: 408 us
  blocking collectives  257 us (63%)
  waiting for transfers between devices  108 us (26%)
  matrix products  18.8 us (5%)
  between operations  14.3 us (4%)
  other arithmetic  6.64 us (2%)
    psum x1, blocking collectives, local(): lax.psum((part_real * unit_scale, part_imag * unit_scale), 'rows')  129 us
    reduce_scatter x1, waiting for transfers between devices, local(): lax.psum_scatter(intensity_part, 'src', scatter_dimension=1, tiled=True)  108 us
    psum x1, blocking collectives, local(): lax.psum((adjoint_real * unit_scale, adjoint_imag * unit_scale), ('src',...  97.3 us
    all_gather x1, blocking collectives, local(): slope = lax.all_gather(slope_share, 'src', axis=1, tiled=True)  30.5 us
    dot_general x12, matrix products, product(): jnp.dot(matrix_left, matrix_right, precision=highest, preferred_element_t...  8.99 us
  transfers between devices with their start and end apart: 1, of which 1 were waited for; matrix products, arithmetic and copies ran while one was open for 0% of the time, Pallas kernels for 0%

commit v1 on v0

--- a/solution.py
+++ b/solution.py
@@ -183,7 +183,7 @@
     adjoint_real = pupil_list[source_point] * back_real
     adjoint_imag = pupil_list[source_point] * back_imag
     adjoint_real, adjoint_imag = lax.psum(
-        (adjoint_real * unit_scale, adjoint_imag * unit_scale), ("src", "rows")
+        lax.psum((adjoint_real * unit_scale, adjoint_imag * unit_scale), "rows"), "src"
     )
     head_real, head_imag = rows_inverse(
         adjoint_real * unit_scale, adjoint_imag * unit_scale, row_start, row_block, total_rows

time: 408 us -> 542 us (1.33)
  blocking collectives: 257 us -> 387 us
    psum x1 -> x2, blocking collectives: 97.3 us -> 228 us  [the longest x1 124 us: local(): lax.psum((adjoint_real * unit_scale, adjoint_imag * unit_scale), 'rows')]
where the time goes in v1:
time: 542 us; the launch traced here: 539 us
  blocking collectives  387 us (71%)
  waiting for transfers between devices  108 us (20%)
  matrix products  18.8 us (3%)
  between operations  14.3 us (3%)
  other arithmetic  6.64 us (1%)
    psum x1, blocking collectives, local(): lax.psum((part_real * unit_scale, part_imag * unit_scale), 'rows')  129 us
    psum x1, blocking collectives, local(): lax.psum((adjoint_real * unit_scale, adjoint_imag * unit_scale), 'rows')  124 us
    reduce_scatter x1, waiting for transfers between devices, local(): lax.psum_scatter(intensity_part, 'src', scatter_dimension=1, tiled=True)  108 us
    psum x1, blocking collectives, local(): lax.psum(lax.psum((adjoint_real * unit_scale, adjoint_imag * unit_scale),...  104 us
    all_gather x1, blocking collectives, local(): slope = lax.all_gather(slope_share, 'src', axis=1, tiled=True)  30.5 us
  transfers between devices with their start and end apart: 1, of which 1 were waited for; matrix products, arithmetic and copies ran while one was open for 0% of the time, Pallas kernels for 0%

profile of v1, /device:TPU:1, one launch (start us, length us, event | category | flops | bytes accessed | tf_op | source)
XLA Modules:
  0.0 538.7 jit_solution(10749562180551666673)
XLA Ops:
  6.5 0.0 reduce-scatter.2.cloned.1.call-start
  6.5 1.2 add_divide_fusion
  7.7 0.1 reshape.193
  7.8 0.1 fusion.73
  8.0 1.5 convolution_negate_fusion
  9.5 0.3 copy.6
  9.9 1.6 add_reduce_fusion.1
  11.4 0.3 fusion.86
  11.8 0.3 fusion.83
  12.1 0.3 fusion.7
  12.4 0.3 fusion.6
  12.8 0.0 copy-start.1
  12.8 0.6 copy-done.1
  13.5 0.6 dynamic_slice.13
  14.0 0.0 copy-start.2
  14.0 0.7 multiply_multiply_fusion.2
  14.7 0.0 copy-done.2
  14.7 0.6 dynamic_slice.12
  15.3 0.7 multiply_multiply_fusion.3
  16.0 128.9 %all-reduce.1 = (f32[32,128]{1,0:T(8,128)S(1)}, f32[32,128]{1,0:T(8,128)S(1)}) all-reduce(f32[32,128]{1,0:T(8,128)S(1)} %fusion.6, f32[32,128]{1,0:T(8,128)S(1)} %fusion.7), channel_id=1, replica_groups=mesh['src'=16,'rows'=32] {'rows'}, use_global_device_ids=true, to_apply=%region_4.5 | all-reduce | flops 8192 | bytes 65536 | tf_op jit(solution)/shard_map/psum | solution.py:156
  144.9 0.2 fusion.37
  145.1 0.3 fusion.38
  145.4 0.3 convolution_subtract_fusion.4
  145.6 0.3 convolution_add_fusion.3
  145.9 1.9 fusion.16
  147.9 1.9 fusion.17
  149.8 0.2 slice_add_fusion
  150.0 0.1 reshape.195
  150.2 0.0 copy-start.3
  150.2 0.1 reshape.196
  150.3 0.5 copy-done.3
  150.8 0.6 reduce_sum.45
  151.4 0.6 broadcast_divide_fusion
  152.1 0.6 dynamic_slice.14
  152.7 1.5 add_multiply_fusion
  154.2 0.0 copy-start
  154.2 0.0 reduce-scatter.2.cloned.1.call-update
  154.8 0.1 fusion.123
  154.9 107.6 %reduce-scatter.2.cloned.1.call-done = f32[16,512]{1,0:T(8,128)} async-done(((f32[16,8192]{1,0:T(8,128)}), f32[16,512]{1,0:T(8,128)}) %reduce-scatter.2.cloned.1.call-update) | async-done | bytes 32784 | tf_op jit(solution)/shard_map/reduce_scatter | solution.py:173
  262.5 0.0 copy-done
  262.5 0.8 subtract_multiply_fusion
  263.3 30.5 %all_gather.3 = f32[16,8192]{1,0:T(8,128)S(1)} all-gather(f32[16,512]{1,0:T(8,128)S(1)} %subtract_multiply_fusion), channel_id=1, replica_groups=mesh['src'=16,'rows'=32] {'src'}, dimensions={1}, use_global_device_ids=true | all-gather | bytes 557056 | tf_op jit(solution)/shard_map/all_gather | solution.py:175
  293.8 0.1 multiply_multiply_fusion
  293.9 0.1 reshape.197
  294.1 0.1 reshape.198
  294.2 1.9 fusion.22
  296.1 1.9 fusion.27
  298.1 0.1 add_reduce_fusion
  298.2 0.3 fusion.80
  298.5 0.3 fusion.77
  298.8 0.3 fusion.5
  299.2 0.3 fusion.3
  299.5 124.2 %all-reduce = (f32[32,128]{1,0:T(8,128)S(1)}, f32[32,128]{1,0:T(8,128)S(1)}) all-reduce(f32[32,128]{1,0:T(8,128)S(1)} %fusion.3, f32[32,128]{1,0:T(8,128)S(1)} %fusion.5), channel_id=1, replica_groups=mesh['src'=16,'rows'=32] {'rows'}, use_global_device_ids=true, to_apply=%region_10.11 | all-reduce | flops 8192 | bytes 65536 | tf_op jit(solution)/shard_map/psum | solution.py:186
  423.7 103.9 %all-reduce.2 = (f32[32,128]{1,0:T(8,128)S(1)}, f32[32,128]{1,0:T(8,128)S(1)}) all-reduce(f32[32,128]{1,0:T(8,128)S(1)} %get-tuple-element.9, f32[32,128]{1,0:T(8,128)S(1)} %get-tuple-element.10), channel_id=1, replica_groups=mesh['src'=16,'rows'=32] {'src'}, use_global_device_ids=true, to_apply=%region_11.12 | all-reduce | flops 8192 | bytes 65536 | tf_op jit(solution)/shard_map/psum | solution.py:185
  527.6 0.3 fusion.35
  527.9 0.3 fusion.31
  528.1 0.3 convolution_subtract_fusion.3
  528.4 0.3 multiply_add_fusion.1
  528.6 1.3 fusion.20
  529.9 1.9 fusion.1
  (7 shorter events, 0.1 us)
Async XLA Ops:
  6.5 256.0 %reduce-scatter.2.cloned.1.call-start = ((), (), s32[]{:S(2)}) async-start(), calls=%async_computation.1 | async-start | bytes 557056 | tf_op jit(solution)/shard_map/reduce_scatter | solution.py:173
  12.8 0.7 copy-start.1
  14.0 0.7 copy-start.2
  150.2 0.7 copy-start.3
  154.2 108.4 %copy-start = (s32[16,512]{1,0:T(8,128)S(1)}, s32[16,512]{1,0:T(8,128)}, u32[]{:S(2)}) copy-start(s32[16,512]{1,0:T(8,128)} %param.6) | copy-start | bytes 98308
Sparse Core Ops, SparseCore 0:
  154.3 108.1 reduce-scatter.1
